TPU v7x, 256 devices: a whole 4x4x8 slice. The times are simulated.
256 devices in a mesh: row: 16 (over z, y_hi), col: 16 (over y_lo, x, core).
Axes of the slice: x: 4, y: 4 (y_hi: 2, y_lo: 2; y = y_hi * 2 + y_lo), z: 8, core: 2. Of those that a mesh axis runs over, the one named last changes fastest.
Arguments:
- source: float32 [131072, 512], P(('row', 'col')), may hold values from -1.3 to 1.3
- context: float32 [131072, 512], P(('row', 'col')), may hold values from -1.3 to 1.3
- pair_counts: int32 [4, 131072, 512], P(None, ('row', 'col')), may hold values from 0 to 4
- partner_masks: int32 [4], replicated, may hold values from 1 to 15, as said below
Outputs:
- source_out: float32 [131072, 512], P(('row', 'col'))
- context_out: float32 [131072, 512], P(('row', 'col'))
Inputs may be any that keep to these rules, and one draw needn't show every extreme that they name: `partner_masks`: entry k is the offset of round k: for even k it is below 16, for odd k below 16; never zero.
All inputs are finite; a program needn't handle non-finite values.
Results may differ from a plain program's by a relative error of at most 0.0019.
Values sent between devices are 32-bit elements; how exact they have to be, the bound alone decides.
A program may use at most 128 MiB of HBM per device.

v0:
```python
import functools

import jax
import jax.numpy as jnp
from jax import lax
from jax.experimental import pallas as pl
from jax.experimental.pallas import tpu as pltpu
from jax.sharding import PartitionSpec as P

LEARN_RATE = 0.05
NEG_WEIGHT = 1.0
EPSILON = 1e-06
MESH = pl.DeviceIdType.MESH
ROWS = 16
COLS = 16
GROUP = 128
PIECES = 8
STRIP = 64


def normalized(param, grad):
    scale = lax.rsqrt(jnp.mean(grad * grad, axis=1, keepdims=True) + EPSILON)
    return param - LEARN_RATE * grad * scale


def place(axis, by):
    row, col = lax.axis_index("row"), lax.axis_index("col")
    if axis == "row":
        return (lax.rem(row + by % ROWS, ROWS), col)
    return (row, lax.rem(col + by % COLS, COLS))


def tiles(count, body):
    def step(i, carry):
        body(i)
        return carry

    lax.fori_loop(0, count, step, 0)


def block(i, size):
    return pl.ds(pl.multiple_of(i * size, size), size)


def source_update(src_ref, coef_ref, low_ref, src_out):
    def step(i):
        rows = block(i, STRIP)
        grad = jnp.dot(coef_ref[rows, :], low_ref[...], preferred_element_type=jnp.float32)
        src_out[rows, :] = normalized(src_ref[rows, :], grad)

    tiles(src_ref.shape[0] // STRIP, step)


def round_kernel(
    axis,
    by,
    turns,
    lap_ref,
    ctx_ref,
    src_in,
    coef_in,
    low_in,
    counts,
    ctx_out,
    src_out,
    coef_out,
    low_out,
    land,
    weight,
    src_low,
    grad_ref,
    send,
    recv,
    wsem,
):
    size = ctx_ref.shape[0]
    piece = size // PIECES
    barrier = pltpu.get_barrier_semaphore()
    pl.semaphore_signal(barrier, inc=1, device_id=place(axis, by), device_id_type=MESH)
    fetches = [
        pltpu.make_async_copy(counts.at[turn], weight.at[lap], wsem.at[lap])
        for lap, turn in enumerate(turns)
    ]
    for fetch in fetches:
        fetch.start()
    pl.semaphore_wait(barrier, 1)

    def move(i):
        rows = pl.ds(pl.multiple_of(i * piece, piece), piece)
        return pltpu.make_async_remote_copy(
            src_ref=ctx_ref.at[rows],
            dst_ref=land.at[rows],
            send_sem=send.at[i],
            recv_sem=recv.at[i],
            device_id=place(axis, -by),
            device_id_type=MESH,
        )

    tiles(PIECES, lambda i: move(i).start())
    source_update(src_in, coef_in, low_in, src_out)

    def narrow(i):
        rows = block(i, STRIP)
        src_low[rows, :] = src_out[rows, :].astype(jnp.bfloat16)

    tiles(size // STRIP, narrow)
    for fetch in fetches:
        fetch.wait()
    lap = lap_ref[0]

    def group(g):
        for k in range(GROUP // piece):
            move(g * (GROUP // piece) + k).wait_recv()
        rows = block(g, GROUP)
        low_out[rows, :] = land[rows, :].astype(jnp.bfloat16)

        def score(i):
            strip = block(i, STRIP)
            scores = lax.dot_general(
                src_low[strip, :],
                low_out[rows, :],
                (((1,), (1,)), ((), ())),
                preferred_element_type=jnp.float32,
            )
            count = weight[lap, strip, rows].astype(jnp.float32)
            coef = (count + NEG_WEIGHT) * jax.nn.sigmoid(scores) - count
            coef_out[strip, rows] = coef.astype(jnp.bfloat16)

        tiles(src_low.shape[0] // STRIP, score)
        grad_ref[...] = lax.dot_general(
            coef_out[:, rows],
            src_low[...],
            (((0,), (0,)), ((), ())),
            preferred_element_type=jnp.float32,
        )

        def update(i):
            strip = pl.ds(pl.multiple_of(g * GROUP + i * 32, 32), 32)
            ctx_out[strip, :] = normalized(land[strip, :], grad_ref[block(i, 32), :])

        tiles(GROUP // 32, update)

    tiles(size // GROUP, group)
    tiles(PIECES, lambda i: move(i).wait_send())


def one_round(axis, by, turns, number, lap, ctx, src, coef, low, counts):
    size, width = ctx.shape
    vmem = pl.BlockSpec(memory_space=pltpu.VMEM)
    out = [jax.ShapeDtypeStruct(x.shape, x.dtype) for x in (ctx, src, coef, low)]
    return pl.pallas_call(
        functools.partial(round_kernel, axis, by, turns),
        out_shape=tuple(out),
        in_specs=[pl.BlockSpec(memory_space=pltpu.SMEM)]
        + [vmem] * 4
        + [pl.BlockSpec(memory_space=pl.ANY)],
        out_specs=[vmem] * 4,
        scratch_shapes=[
            pltpu.VMEM((size, width), jnp.float32),
            pltpu.VMEM((len(turns), src.shape[0], size), jnp.int32),
            pltpu.VMEM(src.shape, jnp.bfloat16),
            pltpu.VMEM((GROUP, width), jnp.float32),
            pltpu.SemaphoreType.DMA((PIECES,)),
            pltpu.SemaphoreType.DMA((PIECES,)),
            pltpu.SemaphoreType.DMA((len(turns),)),
        ],
        name=f"round_{axis}{by}",
        compiler_params=pltpu.CompilerParams(
            collective_id=number, has_side_effects=True, vmem_limit_bytes=24 << 20
        ),
    )(lap, ctx, src, coef, low, counts)


QUARTERS = 4


def return_kernel(by, total, ctx_ref, src_in, coef_in, low_in, ctx_out, src_out, *scratch):
    near = scratch[:QUARTERS]
    stage = scratch[QUARTERS : 2 * QUARTERS]
    far = scratch[2 * QUARTERS : 3 * QUARTERS]
    send1, recv1, send2, recv2 = scratch[3 * QUARTERS :]
    size, width = ctx_ref.shape
    quarter = size // QUARTERS
    piece = quarter // COLS
    row, col = lax.axis_index("row"), lax.axis_index("col")

    def wrap(value, length):
        return lax.rem(value + length, length)

    barrier = pltpu.get_barrier_semaphore()

    def greet(i, carry):
        pl.semaphore_signal(
            barrier, inc=1, device_id=(wrap(row - by, ROWS), wrap(col - i, COLS)), device_id_type=MESH
        )
        return carry

    def greet_col(i, carry):
        pl.semaphore_signal(
            barrier, inc=1, device_id=(row, wrap(col - i, COLS)), device_id_type=MESH
        )
        return carry

    start = 0 if by else 1
    lax.fori_loop(start, COLS, greet, 0)
    if by:
        lax.fori_loop(1, COLS, greet_col, 0)
    pl.semaphore_wait(barrier, COLS - start + (COLS - 1 if by else 0))

    def spread(q, i):
        return pltpu.make_async_remote_copy(
            src_ref=ctx_ref.at[pl.ds(pl.multiple_of(q * quarter + i * piece, piece), piece)],
            dst_ref=near[q].at[i],
            send_sem=send1.at[q],
            recv_sem=recv1.at[q],
            device_id=(wrap(row + by, ROWS), wrap(col + i, COLS)),
            device_id_type=MESH,
        )

    def spread_all(q):
        own = pl.ds(q * quarter + start * piece, quarter - start * piece)
        return pltpu.make_async_remote_copy(
            src_ref=ctx_ref.at[own],
            dst_ref=near[q].at[pl.ds(start, COLS - start)],
            send_sem=send1.at[q],
            recv_sem=recv1.at[q],
            device_id=(wrap(row + by, ROWS), wrap(col + 1, COLS)),
            device_id_type=MESH,
        )

    def deliver_all(q):
        return pltpu.make_async_remote_copy(
            src_ref=stage[q].at[pl.ds(1, COLS - 1)],
            dst_ref=far[q].at[pl.ds(1, COLS - 1)],
            send_sem=send2.at[q],
            recv_sem=recv2.at[q],
            device_id=(row, wrap(col + 1, COLS)),
            device_id_type=MESH,
        )

    def deliver(q, i):
        return pltpu.make_async_remote_copy(
            src_ref=stage[q].at[i],
            dst_ref=far[q].at[i],
            send_sem=send2.at[q],
            recv_sem=recv2.at[q],
            device_id=(row, wrap(col + i, COLS)),
            device_id_type=MESH,
        )

    def begin(q):
        tiles(COLS - start, lambda i: spread(q, i + start).start())
        if not by:
            near[q][0] = ctx_ref[pl.ds(q * quarter, piece), :]

    begin(0)
    begin(1)
    source_update(src_in, coef_in, low_in, src_out)
    shift = total[0]
    for q in range(QUARTERS):
        spread_all(q).wait_recv()
        if q + 2 < QUARTERS:
            begin(q + 2)
        far[q][0] = near[q][lax.rem(shift, COLS)]

        def pass_on(i, q=q):
            stage[q][i + 1] = near[q][lax.rem(shift - i - 1 + COLS, COLS)]
            deliver(q, i + 1).start()

        tiles(COLS - 1, pass_on)
    for q in range(QUARTERS):
        deliver_all(q).wait_recv()

        def settle(i, q=q):
            rows = pl.ds(pl.multiple_of(q * quarter + i * piece, piece), piece)
            ctx_out[rows, :] = far[q][lax.rem(shift - i + COLS, COLS)]

        tiles(COLS, settle)
    for q in range(QUARTERS):
        deliver_all(q).wait_send()
        spread_all(q).wait_send()


def go_home(by, number, total, ctx, src, coef, low):
    size, width = ctx.shape
    quarter = size // QUARTERS
    vmem = pl.BlockSpec(memory_space=pltpu.VMEM)
    full = jax.ShapeDtypeStruct((size, width), jnp.float32)
    slots = pltpu.VMEM((COLS, quarter // COLS, width), jnp.float32)
    return pl.pallas_call(
        functools.partial(return_kernel, by),
        out_shape=(full, full),
        in_specs=[pl.BlockSpec(memory_space=pltpu.SMEM)] + [vmem] * 4,
        out_specs=[vmem] * 2,
        scratch_shapes=[slots] * (3 * QUARTERS) + [pltpu.SemaphoreType.DMA((QUARTERS,))] * 4,
        name=f"home{by}",
        compiler_params=pltpu.CompilerParams(
            collective_id=number, has_side_effects=True, vmem_limit_bytes=24 << 20
        ),
    )(total, ctx, src, coef, low)


def per_device(source, context, pair_counts, partner_masks):
    rounds = pair_counts.shape[0]

    def both(lap, carried):
        for half, (axis, length) in enumerate((("row", ROWS), ("col", COLS))):
            branches = [
                functools.partial(
                    one_round, axis, by, range(half, rounds, 2), half * ROWS + by
                )
                for by in range(1, length)
            ]
            carried = lax.switch(
                partner_masks[2 * lap + half] - 1,
                branches,
                lap.reshape(1),
                *carried,
                pair_counts,
            )
        return tuple(carried)

    coef = jnp.zeros((source.shape[0], context.shape[0]), jnp.bfloat16)
    low = jnp.zeros(context.shape, jnp.bfloat16)
    ctx, src, coef, low = lax.fori_loop(0, rounds // 2, both, (context, source, coef, low))
    row_total = sum(partner_masks[turn] for turn in range(0, rounds, 2)) % ROWS
    col_total = sum(partner_masks[turn] for turn in range(1, rounds, 2)) % COLS
    branches = [functools.partial(go_home, by, 2 * ROWS + by) for by in range(ROWS)]
    ctx, src = lax.switch(row_total, branches, col_total.reshape(1), ctx, src, coef, low)
    return (src, ctx)


def solution(mesh):
    in_specs = (
        P(("row", "col"), None),
        P(("row", "col"), None),
        P(None, ("row", "col"), None),
        P(),
    )
    out_specs = (P(("row", "col"), None), P(("row", "col"), None))
    return jax.shard_map(
        per_device, mesh=mesh, in_specs=in_specs, out_specs=out_specs, check_vma=False
    )
```

profile of v0, /device:TPU:1, one launch (start us, length us, event | category | flops | bytes accessed | tf_op | source)
XLA Modules:
  0.0 189.7 jit_solution(4519605183524938580)
XLA Ops:
  0.6 0.0 copy-start
  0.6 2.3 %copy.178 = f32[512,512]{1,0:T(8,128)} copy(f32[512,512]{1,0:T(8,128)} %param.53) | data formatting | bytes 2097152
  2.9 2.3 %copy.177 = f32[512,512]{1,0:T(8,128)} copy(f32[512,512]{1,0:T(8,128)} %param.52) | data formatting | bytes 2097152
  5.2 0.0 copy-done
  5.2 0.6 fusion.1
  8.3 0.8 broadcast.5.clone
  9.2 0.8 broadcast.5
  10.0 134.8 %while.22 = (s32[]{:T(128)}, f32[512,512]{1,0:T(8,128)}, f32[512,512]{1,0:T(8,128)}, bf16[512,512]{1,0:T(8,128)(2,1)}, bf16[512,512]{1,0:T(8,128)(2,1)}, /*index...) while((s32[]{:T(128)}, f32[512,512]{1,0:T(8,128)}, ...), condition=%wide.region_31.0_spmd, body=%wide.region_0.0_spmd.sunk | while | flops 14 | bytes 433 | solution.py:325
  10.0 0.6 fusion.3
  11.8 53.2 %conditional.6 = ((f32[512,512]{1,0:T(8,128)S(1)}, f32[512,512]{1,0:T(8,128)S(1)}, bf16[512,512]{1,0:T(8,128)(2,1)S(1)}, bf16[512,512]{1,0:T(8,128)(2,1)S(1)})) conditional(s32[]{:T(128)} %bitcast.11, (s32[1]{0:T(128)}, f32[512,512]{1,0:T(8,128)}, f32[512,512]{1,0:T(8,128)}, bf16[512,512]{1,0:T(8,128)(2,1)}, ...), branch_computations={%region_1.0_spmd, %region_2.0_spmd, %region_3.0_spmd, %region_4.0_... | conditional | bytes 8 | solution.py:314
  11.8 53.2 %round_row3.1 = (f32[512,512]{1,0:T(8,128)S(1)}, f32[512,512]{1,0:T(8,128)S(1)}, bf16[512,512]{1,0:T(8,128)(2,1)S(1)}, bf16[512,512]{1,0:T(8,128)(2,1)S(1)}) custom-call(s32[1]{0:T(128)} %get-tuple-element.746.lap_ref, f32[512,512]{1,0:T(8,128)} %get-tuple-element.747.ctx_ref, f32[512,512]{1,0:T(8,128)} %get-tuple-element.748.src_in, ...), custom_call_target="tpu_custom_call" | custom-call | tf_op jit(solution)/shard_map/while/body/eval_jaxpr/cond/branch_2_fun/round_row3/pallas_call | solution.py:151
  65.1 21.3 %conditional.7 = ((f32[512,512]{1,0:T(8,128)}, f32[512,512]{1,0:T(8,128)}, bf16[512,512]{1,0:T(8,128)(2,1)}, bf16[512,512]{1,0:T(8,128)(2,1)})) conditional(s32[]{:T(128)} %bitcast.9, (s32[1]{0:T(128)}, f32[512,512]{1,0:T(8,128)S(1)}, f32[512,512]{1,0:T(8,128)S(1)}, bf16[512,512]{1,0:T(8,128)(2,1)S(1)}, ...), branch_computations={%region_16.0_spmd, %region_17.0_spmd, %region_18.0_spmd, %region_1... | conditional | bytes 8 | solution.py:314
  65.1 21.2 %round_col7.1 = (f32[512,512]{1,0:T(8,128)}, f32[512,512]{1,0:T(8,128)}, bf16[512,512]{1,0:T(8,128)(2,1)}, bf16[512,512]{1,0:T(8,128)(2,1)}) custom-call(s32[1]{0:T(128)} %get-tuple-element.860.lap_ref, f32[512,512]{1,0:T(8,128)S(1)} %get-tuple-element.861.ctx_ref, f32[512,512]{1,0:T(8,128)S(1)} %get-tuple-element.862.src_in, ...), custom_call_target="tpu_custom_call" | custom-call | tf_op jit(solution)/shard_map/while/body/eval_jaxpr/cond/branch_6_fun/round_col7/pallas_call | solution.py:151
  86.4 0.6 fusion.3
  88.2 33.8 %conditional.6 = ((f32[512,512]{1,0:T(8,128)S(1)}, f32[512,512]{1,0:T(8,128)S(1)}, bf16[512,512]{1,0:T(8,128)(2,1)S(1)}, bf16[512,512]{1,0:T(8,128)(2,1)S(1)})) conditional(s32[]{:T(128)} %bitcast.11, (s32[1]{0:T(128)}, f32[512,512]{1,0:T(8,128)}, f32[512,512]{1,0:T(8,128)}, bf16[512,512]{1,0:T(8,128)(2,1)}, ...), branch_computations={%region_1.0_spmd, %region_2.0_spmd, %region_3.0_spmd, %region_4.0_... | conditional | bytes 8 | solution.py:314
  88.2 33.7 %round_row15.1 = (f32[512,512]{1,0:T(8,128)S(1)}, f32[512,512]{1,0:T(8,128)S(1)}, bf16[512,512]{1,0:T(8,128)(2,1)S(1)}, bf16[512,512]{1,0:T(8,128)(2,1)S(1)}) custom-call(s32[1]{0:T(128)} %get-tuple-element.818.lap_ref, f32[512,512]{1,0:T(8,128)} %get-tuple-element.819.ctx_ref, f32[512,512]{1,0:T(8,128)} %get-tuple-element.820.src_in, ...), custom_call_target="tpu_custom_call" | custom-call | tf_op jit(solution)/shard_map/while/body/eval_jaxpr/cond/branch_14_fun/round_row15/pallas_call | solution.py:151
  121.9 22.9 %conditional.7 = ((f32[512,512]{1,0:T(8,128)}, f32[512,512]{1,0:T(8,128)}, bf16[512,512]{1,0:T(8,128)(2,1)}, bf16[512,512]{1,0:T(8,128)(2,1)})) conditional(s32[]{:T(128)} %bitcast.9, (s32[1]{0:T(128)}, f32[512,512]{1,0:T(8,128)S(1)}, f32[512,512]{1,0:T(8,128)S(1)}, bf16[512,512]{1,0:T(8,128)(2,1)S(1)}, ...), branch_computations={%region_16.0_spmd, %region_17.0_spmd, %region_18.0_spmd, %region_1... | conditional | bytes 8 | solution.py:314
  122.0 22.8 %round_col15.1 = (f32[512,512]{1,0:T(8,128)}, f32[512,512]{1,0:T(8,128)}, bf16[512,512]{1,0:T(8,128)(2,1)}, bf16[512,512]{1,0:T(8,128)(2,1)}) custom-call(s32[1]{0:T(128)} %get-tuple-element.908.lap_ref, f32[512,512]{1,0:T(8,128)S(1)} %get-tuple-element.909.ctx_ref, f32[512,512]{1,0:T(8,128)S(1)} %get-tuple-element.910.src_in, ...), custom_call_target="tpu_custom_call" | custom-call | tf_op jit(solution)/shard_map/while/body/eval_jaxpr/cond/branch_14_fun/round_col15/pallas_call | solution.py:151
  144.8 43.0 %conditional.3 = ((f32[512,512]{1,0:T(8,128)S(1)}, f32[512,512]{1,0:T(8,128)S(1)})) conditional(s32[]{:T(128)} %clamp.31, (s32[1]{0:T(128)}, f32[512,512]{1,0:T(8,128)}, f32[512,512]{1,0:T(8,128)}, bf16[512,512]{1,0:T(8,128)(2,1)}, bf16[512,512]{1,0:T(8,128)(2,1)}) %tuple.172, (s32[1]{0:T(128)}, ...), branch_computations={%region_32.33_spmd, %region_33.34_spmd, %region_34.35_spmd, %regio... | conditional | bytes 8 | solution.py:329
  144.9 42.7 %home2.1 = (f32[512,512]{1,0:T(8,128)S(1)}, f32[512,512]{1,0:T(8,128)S(1)}) custom-call(s32[1]{0:T(128)} %get-tuple-element.940.total, f32[512,512]{1,0:T(8,128)} %get-tuple-element.941.ctx_ref, f32[512,512]{1,0:T(8,128)} %get-tuple-element.942.src_in, bf16[512,512]{1,0:T(8,128)(2,1)} %get-tuple-element.943.coef_in, bf16[512,512]{1,0:T(8,128)(2,1)} %get-tuple-element.944.low_in), custom_call_target="tpu_custom_call" | custom-call | tf_op jit(solution)/shard_map/cond/branch_2_fun/home2/pallas_call | solution.py:290
  187.8 1.0 copy.179
  188.7 1.0 copy.180
Async XLA Ops:
  0.6 4.6 %copy-start = (s32[4]{0:T(128)S(1)}, s32[4]{0:T(128)}, u32[]{:S(2)}) copy-start(s32[4]{0:T(128)} %param.55) | copy-start | bytes 52
where the time goes:
time: 190 us
  Pallas kernels  174 us (92%)
  local copies, waits for them, and re-layouts  10 us (5%)
  between operations  3.17 us (2%)
  loops' own time  2.91 us (2%)
    pallas_call x4, Pallas kernels, one_round(): pl.pallas_call(functools.partial(round_kernel, axis, by, turns), out_shap...  131 us
    pallas_call x1, Pallas kernels, go_home(): pl.pallas_call(functools.partial(return_kernel, by), out_shape=(full, ful...  42.7 us
    unnamed x6, local copies, waits for them, and re-layouts  6.51 us

commit v1 on v0

--- a/solution.py
+++ b/solution.py
@@ -14,7 +14,7 @@
 ROWS = 16
 COLS = 16
 GROUP = 128
-PIECES = 8
+PIECES = 16
 STRIP = 64
 
 
@@ -26,8 +26,27 @@
 def place(axis, by):
     row, col = lax.axis_index("row"), lax.axis_index("col")
     if axis == "row":
-        return (lax.rem(row + by % ROWS, ROWS), col)
-    return (row, lax.rem(col + by % COLS, COLS))
+        return (lax.rem(row + by + ROWS, ROWS), col)
+    return (row, lax.rem(col + by + COLS, COLS))
+
+
+class Detour:
+    def __init__(self, shift, parts):
+        counts, first, second = [], [], []
+        for odd in range(2):
+            hops = ((odd + shift) // 2) % 8
+            hops = hops - 8 if hops > 4 else hops
+            sign = 1 if hops > 0 else -1
+            leg = {2: -3 * sign, 3: -2 * sign}.get(abs(hops), 0)
+            counts.append({2: parts[0], 3: parts[1]}.get(abs(hops), 0))
+            first.append(2 * leg % ROWS)
+            second.append((shift - 2 * leg) % ROWS)
+        self.shift, self.counts, self.first, self.second = shift, counts, first, second
+        self.any = max(counts) > 0
+
+    @staticmethod
+    def pick(values, odd):
+        return values[0] if values[0] == values[1] else values[0] + (values[1] - values[0]) * odd
 
 
 def tiles(count, body):
@@ -49,6 +68,17 @@
         src_out[rows, :] = normalized(src_ref[rows, :], grad)
 
     tiles(src_ref.shape[0] // STRIP, step)
+
+
+def as_flag(count):
+    return jnp.minimum(count, 1)
+
+
+def detour_of(axis, by):
+    if axis != "row":
+        return None
+    detour = Detour(-by, (4, 6))
+    return detour if detour.any else None
 
 
 def round_kernel(
@@ -72,18 +102,39 @@
     send,
     recv,
     wsem,
+    hop=None,
+    hop_send=None,
+    hop_recv=None,
 ):
     size = ctx_ref.shape[0]
     piece = size // PIECES
-    barrier = pltpu.get_barrier_semaphore()
-    pl.semaphore_signal(barrier, inc=1, device_id=place(axis, by), device_id_type=MESH)
     fetches = [
         pltpu.make_async_copy(counts.at[turn], weight.at[lap], wsem.at[lap])
         for lap, turn in enumerate(turns)
     ]
     for fetch in fetches:
         fetch.start()
-    pl.semaphore_wait(barrier, 1)
+    detour = detour_of(axis, by)
+    barrier = pltpu.get_barrier_semaphore()
+
+    def greet(there):
+        pl.semaphore_signal(barrier, inc=1, device_id=there, device_id_type=MESH)
+
+    greet(place(axis, by))
+    long = 0
+    if detour is None:
+        pl.semaphore_wait(barrier, 1)
+    else:
+        odd = lax.rem(lax.axis_index("row"), 2)
+        origin = lax.rem(odd + by, 2)
+        long = detour.pick(detour.counts, odd)
+        first, second = detour.pick(detour.first, odd), detour.pick(detour.second, odd)
+        tiles(as_flag(long), lambda i: greet(place(axis, ROWS - first)))
+        tiles(
+            as_flag(detour.pick(detour.counts, origin)),
+            lambda i: greet(place(axis, ROWS - detour.pick(detour.second, origin))),
+        )
+        pl.semaphore_wait(barrier, 1 + 2 * as_flag(long))
 
     def move(i):
         rows = pl.ds(pl.multiple_of(i * piece, piece), piece)
@@ -96,7 +147,29 @@
             device_id_type=MESH,
         )
 
-    tiles(PIECES, lambda i: move(i).start())
+    def depart(i):
+        return pltpu.make_async_remote_copy(
+            src_ref=ctx_ref.at[block(PIECES - long + i, piece)],
+            dst_ref=hop.at[block(i, piece)],
+            send_sem=send.at[PIECES - long + i],
+            recv_sem=hop_recv.at[i],
+            device_id=place(axis, first),
+            device_id_type=MESH,
+        )
+
+    def forward(i):
+        return pltpu.make_async_remote_copy(
+            src_ref=hop.at[block(i, piece)],
+            dst_ref=land.at[block(PIECES - long + i, piece)],
+            send_sem=hop_send.at[i],
+            recv_sem=recv.at[PIECES - long + i],
+            device_id=place(axis, second),
+            device_id_type=MESH,
+        )
+
+    if detour is not None:
+        tiles(long, lambda i: depart(i).start())
+    tiles(PIECES - long, lambda i: move(i).start())
     source_update(src_in, coef_in, low_in, src_out)
 
     def narrow(i):
@@ -109,8 +182,7 @@
     lap = lap_ref[0]
 
     def group(g):
-        for k in range(GROUP // piece):
-            move(g * (GROUP // piece) + k).wait_recv()
+        tiles(GROUP // piece, lambda k: move(g * (GROUP // piece) + k).wait_recv())
         rows = block(g, GROUP)
         low_out[rows, :] = land[rows, :].astype(jnp.bfloat16)
 
@@ -140,14 +212,32 @@
 
         tiles(GROUP // 32, update)
 
+    if detour is not None:
+
+        def relay(i):
+            depart(i).wait_recv()
+            forward(i).start()
+
+        tiles(long, relay)
     tiles(size // GROUP, group)
     tiles(PIECES, lambda i: move(i).wait_send())
+    if detour is not None:
+        tiles(long, lambda i: forward(i).wait_send())
 
 
 def one_round(axis, by, turns, number, lap, ctx, src, coef, low, counts):
     size, width = ctx.shape
     vmem = pl.BlockSpec(memory_space=pltpu.VMEM)
     out = [jax.ShapeDtypeStruct(x.shape, x.dtype) for x in (ctx, src, coef, low)]
+    detour = detour_of(axis, by)
+    detour_scratch = []
+    if detour is not None:
+        most = max(detour.counts)
+        detour_scratch = [
+            pltpu.VMEM((most * (size // PIECES), width), jnp.float32),
+            pltpu.SemaphoreType.DMA((most,)),
+            pltpu.SemaphoreType.DMA((most,)),
+        ]
     return pl.pallas_call(
         functools.partial(round_kernel, axis, by, turns),
         out_shape=tuple(out),
@@ -163,7 +253,8 @@
             pltpu.SemaphoreType.DMA((PIECES,)),
             pltpu.SemaphoreType.DMA((PIECES,)),
             pltpu.SemaphoreType.DMA((len(turns),)),
-        ],
+        ]
+        + detour_scratch,
         name=f"round_{axis}{by}",
         compiler_params=pltpu.CompilerParams(
             collective_id=number, has_side_effects=True, vmem_limit_bytes=24 << 20
@@ -174,38 +265,50 @@
 QUARTERS = 4
 
 
+def home_detour(by):
+    detour = Detour(by, (COLS, COLS + COLS // 2))
+    return detour if detour.any else None
+
+
 def return_kernel(by, total, ctx_ref, src_in, coef_in, low_in, ctx_out, src_out, *scratch):
     near = scratch[:QUARTERS]
     stage = scratch[QUARTERS : 2 * QUARTERS]
     far = scratch[2 * QUARTERS : 3 * QUARTERS]
-    send1, recv1, send2, recv2 = scratch[3 * QUARTERS :]
+    send1, recv1, send2, recv2, *detoured = scratch[3 * QUARTERS :]
     size, width = ctx_ref.shape
     quarter = size // QUARTERS
     piece = quarter // COLS
     row, col = lax.axis_index("row"), lax.axis_index("col")
 
-    def wrap(value, length):
-        return lax.rem(value + length, length)
+    def at(row_by, col_by):
+        return (lax.rem(row + row_by + ROWS, ROWS), lax.rem(col + col_by + COLS, COLS))
 
     barrier = pltpu.get_barrier_semaphore()
 
-    def greet(i, carry):
-        pl.semaphore_signal(
-            barrier, inc=1, device_id=(wrap(row - by, ROWS), wrap(col - i, COLS)), device_id_type=MESH
-        )
-        return carry
-
-    def greet_col(i, carry):
-        pl.semaphore_signal(
-            barrier, inc=1, device_id=(row, wrap(col - i, COLS)), device_id_type=MESH
-        )
-        return carry
+    def greet(there):
+        pl.semaphore_signal(barrier, inc=1, device_id=there, device_id_type=MESH)
 
     start = 0 if by else 1
-    lax.fori_loop(start, COLS, greet, 0)
+    tiles(COLS - start, lambda i: greet(at(-by, -i - start)))
     if by:
-        lax.fori_loop(1, COLS, greet_col, 0)
-    pl.semaphore_wait(barrier, COLS - start + (COLS - 1 if by else 0))
+        tiles(COLS - 1, lambda i: greet(at(0, -i - 1)))
+    met = COLS - start + (COLS - 1 if by else 0)
+    detour = home_detour(by)
+    long = 0
+    if detour is not None:
+        hop, hop_send, hop_recv = detoured
+        odd = lax.rem(row, 2)
+        origin = lax.rem(odd + by, 2)
+        long = detour.pick(detour.counts, odd)
+        first, second = detour.pick(detour.first, odd), detour.pick(detour.second, odd)
+        tiles(as_flag(long), lambda i: greet(at(-first, 0)))
+        back = detour.pick(detour.second, origin)
+        tiles(
+            as_flag(detour.pick(detour.counts, origin)) * COLS,
+            lambda i: greet(at(-back, -i)),
+        )
+        met = met + (COLS + 1) * as_flag(long)
+    pl.semaphore_wait(barrier, met)
 
     def spread(q, i):
         return pltpu.make_async_remote_copy(
@@ -213,7 +316,7 @@
             dst_ref=near[q].at[i],
             send_sem=send1.at[q],
             recv_sem=recv1.at[q],
-            device_id=(wrap(row + by, ROWS), wrap(col + i, COLS)),
+            device_id=at(by, i),
             device_id_type=MESH,
         )
 
@@ -224,7 +327,7 @@
             dst_ref=near[q].at[pl.ds(start, COLS - start)],
             send_sem=send1.at[q],
             recv_sem=recv1.at[q],
-            device_id=(wrap(row + by, ROWS), wrap(col + 1, COLS)),
+            device_id=at(by, 1),
             device_id_type=MESH,
         )
 
@@ -234,7 +337,7 @@
             dst_ref=far[q].at[pl.ds(1, COLS - 1)],
             send_sem=send2.at[q],
             recv_sem=recv2.at[q],
-            device_id=(row, wrap(col + 1, COLS)),
+            device_id=at(0, 1),
             device_id_type=MESH,
         )
 
@@ -244,23 +347,66 @@
             dst_ref=far[q].at[i],
             send_sem=send2.at[q],
             recv_sem=recv2.at[q],
-            device_id=(row, wrap(col + i, COLS)),
-            device_id_type=MESH,
-        )
-
-    def begin(q):
-        tiles(COLS - start, lambda i: spread(q, i + start).start())
+            device_id=at(0, i),
+            device_id_type=MESH,
+        )
+
+    half = quarter // 2
+
+    def depart(q, part):
+        return pltpu.make_async_remote_copy(
+            src_ref=ctx_ref.at[pl.ds(q * quarter + part * half, half)],
+            dst_ref=hop[q % 2].at[pl.ds(part * half, half)],
+            send_sem=send1.at[q],
+            recv_sem=hop_recv.at[q % 2 * 2 + part],
+            device_id=at(first, 0),
+            device_id_type=MESH,
+        )
+
+    def relay(q, part, i):
+        return pltpu.make_async_remote_copy(
+            src_ref=hop[q % 2].at[pl.ds(pl.multiple_of(i * piece, piece), piece)],
+            dst_ref=near[q].at[i],
+            send_sem=hop_send.at[q % 2 * 2 + part],
+            recv_sem=recv1.at[q],
+            device_id=at(second, i),
+            device_id_type=MESH,
+        )
+
+    def relayed(q, part):
+        return pltpu.make_async_remote_copy(
+            src_ref=hop[q % 2].at[pl.ds(part * half, half)],
+            dst_ref=near[q].at[pl.ds(part * (COLS // 2), COLS // 2)],
+            send_sem=hop_send.at[q % 2 * 2 + part],
+            recv_sem=recv1.at[q],
+            device_id=at(second, 1),
+            device_id_type=MESH,
+        )
+
+    ways = []
+    if detour is not None:
+        ways = [(3, 0, as_flag(long)), (3, 1, as_flag(long)), (2, 1, as_flag(long // (COLS + 1)))]
+    for q, part, flag in ways:
+        tiles(flag, lambda i, q=q, part=part: depart(q, part).start())
+    for q in range(QUARTERS):
+        direct = COLS - start
+        for other, part, flag in ways:
+            if other == q:
+                direct = direct - flag * (COLS // 2)
+        tiles(direct, lambda i, q=q: spread(q, i + start).start())
         if not by:
             near[q][0] = ctx_ref[pl.ds(q * quarter, piece), :]
-
-    begin(0)
-    begin(1)
     source_update(src_in, coef_in, low_in, src_out)
+    for q, part, flag in ways:
+
+        def pass_relay(i, q=q, part=part):
+            depart(q, part).wait_recv()
+            tiles(COLS // 2, lambda k: relay(q, part, part * (COLS // 2) + k).start())
+
+        tiles(flag, pass_relay)
     shift = total[0]
     for q in range(QUARTERS):
         spread_all(q).wait_recv()
-        if q + 2 < QUARTERS:
-            begin(q + 2)
         far[q][0] = near[q][lax.rem(shift, COLS)]
 
         def pass_on(i, q=q):
@@ -279,6 +425,8 @@
     for q in range(QUARTERS):
         deliver_all(q).wait_send()
         spread_all(q).wait_send()
+    for q, part, flag in ways:
+        tiles(flag, lambda i, q=q, part=part: relayed(q, part).wait_send())
 
 
 def go_home(by, number, total, ctx, src, coef, low):
@@ -287,12 +435,21 @@
     vmem = pl.BlockSpec(memory_space=pltpu.VMEM)
     full = jax.ShapeDtypeStruct((size, width), jnp.float32)
     slots = pltpu.VMEM((COLS, quarter // COLS, width), jnp.float32)
+    detoured = []
+    if home_detour(by) is not None:
+        detoured = [
+            [pltpu.VMEM((quarter, width), jnp.float32)] * 2,
+            pltpu.SemaphoreType.DMA((4,)),
+            pltpu.SemaphoreType.DMA((4,)),
+        ]
     return pl.pallas_call(
         functools.partial(return_kernel, by),
         out_shape=(full, full),
         in_specs=[pl.BlockSpec(memory_space=pltpu.SMEM)] + [vmem] * 4,
         out_specs=[vmem] * 2,
-        scratch_shapes=[slots] * (3 * QUARTERS) + [pltpu.SemaphoreType.DMA((QUARTERS,))] * 4,
+        scratch_shapes=[slots] * (3 * QUARTERS)
+        + [pltpu.SemaphoreType.DMA((QUARTERS,))] * 4
+        + detoured,
         name=f"home{by}",
         compiler_params=pltpu.CompilerParams(
             collective_id=number, has_side_effects=True, vmem_limit_bytes=24 << 20

time: 190 us -> 227 us (1.19)
  Pallas kernels: 174 us -> 211 us
    pallas_call x1, Pallas kernels: 42.7 us -> 75.6 us  [go_home(): pl.pallas_call(functools.partial(return_kernel, by), out_shape=(full, ful...]
    pallas_call x4, Pallas kernels: 131 us -> 136 us  [one_round(): pl.pallas_call(functools.partial(round_kernel, axis, by, turns), out_shap...]
where the time goes in v1:
time: 227 us
  Pallas kernels  211 us (93%)
  local copies, waits for them, and re-layouts  10 us (4%)
  between operations  3.17 us (1%)
  loops' own time  2.91 us (1%)
    pallas_call x4, Pallas kernels, one_round(): pl.pallas_call(functools.partial(round_kernel, axis, by, turns), out_shap...  136 us
    pallas_call x1, Pallas kernels, go_home(): pl.pallas_call(functools.partial(return_kernel, by), out_shape=(full, ful...  75.6 us
    unnamed x6, local copies, waits for them, and re-layouts  6.51 us

profile of v1, /device:TPU:1, one launch (start us, length us, event | category | flops | bytes accessed | tf_op | source)
XLA Modules:
  0.0 227.2 jit_solution(2306090267586387935)
XLA Ops:
  0.6 0.0 copy-start
  0.6 2.3 copy.178
  2.9 2.3 %copy.177 = f32[512,512]{1,0:T(8,128)} copy(f32[512,512]{1,0:T(8,128)} %param.52) | data formatting | bytes 2097152
  5.2 0.0 copy-done
  5.2 0.6 fusion.1
  8.3 0.8 broadcast.5.clone
  9.2 0.8 broadcast.5
  10.0 139.6 %while.22 = (s32[]{:T(128)}, f32[512,512]{1,0:T(8,128)}, f32[512,512]{1,0:T(8,128)}, bf16[512,512]{1,0:T(8,128)(2,1)}, bf16[512,512]{1,0:T(8,128)(2,1)}, /*index...) while((s32[]{:T(128)}, f32[512,512]{1,0:T(8,128)}, ...), condition=%wide.region_31.0_spmd, body=%wide.region_0.0_spmd.sunk | while | flops 14 | bytes 433 | solution.py:482
  10.0 0.6 fusion.3
  11.8 33.7 %conditional.6 = ((f32[512,512]{1,0:T(8,128)S(1)}, f32[512,512]{1,0:T(8,128)S(1)}, bf16[512,512]{1,0:T(8,128)(2,1)S(1)}, bf16[512,512]{1,0:T(8,128)(2,1)S(1)})) conditional(s32[]{:T(128)} %bitcast.11, (s32[1]{0:T(128)}, f32[512,512]{1,0:T(8,128)}, f32[512,512]{1,0:T(8,128)}, bf16[512,512]{1,0:T(8,128)(2,1)}, ...), branch_computations={%region_1.0_spmd, %region_2.0_spmd, %region_3.0_spmd, %region_4.0_... | conditional | bytes 8 | solution.py:471
  11.9 33.6 %round_row14.1 = (f32[512,512]{1,0:T(8,128)S(1)}, f32[512,512]{1,0:T(8,128)S(1)}, bf16[512,512]{1,0:T(8,128)(2,1)S(1)}, bf16[512,512]{1,0:T(8,128)(2,1)S(1)}) custom-call(s32[1]{0:T(128)} %get-tuple-element.812.lap_ref, f32[512,512]{1,0:T(8,128)} %get-tuple-element.813.ctx_ref, f32[512,512]{1,0:T(8,128)} %get-tuple-element.814.src_in, ...), custom_call_target="tpu_custom_call" | custom-call | tf_op jit(solution)/shard_map/while/body/eval_jaxpr/cond/branch_13_fun/round_row14/pallas_call | solution.py:241
  45.5 16.1 %conditional.7 = ((f32[512,512]{1,0:T(8,128)}, f32[512,512]{1,0:T(8,128)}, bf16[512,512]{1,0:T(8,128)(2,1)}, bf16[512,512]{1,0:T(8,128)(2,1)})) conditional(s32[]{:T(128)} %bitcast.9, (s32[1]{0:T(128)}, f32[512,512]{1,0:T(8,128)S(1)}, f32[512,512]{1,0:T(8,128)S(1)}, bf16[512,512]{1,0:T(8,128)(2,1)S(1)}, ...), branch_computations={%region_16.0_spmd, %region_17.0_spmd, %region_18.0_spmd, %region_1... | conditional | bytes 8 | solution.py:471
  45.5 16.1 %round_col15.1 = (f32[512,512]{1,0:T(8,128)}, f32[512,512]{1,0:T(8,128)}, bf16[512,512]{1,0:T(8,128)(2,1)}, bf16[512,512]{1,0:T(8,128)(2,1)}) custom-call(s32[1]{0:T(128)} %get-tuple-element.908.lap_ref, f32[512,512]{1,0:T(8,128)S(1)} %get-tuple-element.909.ctx_ref, f32[512,512]{1,0:T(8,128)S(1)} %get-tuple-element.910.src_in, ...), custom_call_target="tpu_custom_call" | custom-call | tf_op jit(solution)/shard_map/while/body/eval_jaxpr/cond/branch_14_fun/round_col15/pallas_call | solution.py:241
  61.6 0.6 fusion.3
  63.4 50.5 %conditional.6 = ((f32[512,512]{1,0:T(8,128)S(1)}, f32[512,512]{1,0:T(8,128)S(1)}, bf16[512,512]{1,0:T(8,128)(2,1)S(1)}, bf16[512,512]{1,0:T(8,128)(2,1)S(1)})) conditional(s32[]{:T(128)} %bitcast.11, (s32[1]{0:T(128)}, f32[512,512]{1,0:T(8,128)}, f32[512,512]{1,0:T(8,128)}, bf16[512,512]{1,0:T(8,128)(2,1)}, ...), branch_computations={%region_1.0_spmd, %region_2.0_spmd, %region_3.0_spmd, %region_4.0_... | conditional | bytes 8 | solution.py:471
  63.5 50.5 %round_row11.1 = (f32[512,512]{1,0:T(8,128)S(1)}, f32[512,512]{1,0:T(8,128)S(1)}, bf16[512,512]{1,0:T(8,128)(2,1)S(1)}, bf16[512,512]{1,0:T(8,128)(2,1)S(1)}) custom-call(s32[1]{0:T(128)} %get-tuple-element.794.lap_ref, f32[512,512]{1,0:T(8,128)} %get-tuple-element.795.ctx_ref, f32[512,512]{1,0:T(8,128)} %get-tuple-element.796.src_in, ...), custom_call_target="tpu_custom_call" | custom-call | tf_op jit(solution)/shard_map/while/body/eval_jaxpr/cond/branch_10_fun/round_row11/pallas_call | solution.py:241
  114.0 35.4 %conditional.7 = ((f32[512,512]{1,0:T(8,128)}, f32[512,512]{1,0:T(8,128)}, bf16[512,512]{1,0:T(8,128)(2,1)}, bf16[512,512]{1,0:T(8,128)(2,1)})) conditional(s32[]{:T(128)} %bitcast.9, (s32[1]{0:T(128)}, f32[512,512]{1,0:T(8,128)S(1)}, f32[512,512]{1,0:T(8,128)S(1)}, bf16[512,512]{1,0:T(8,128)(2,1)S(1)}, ...), branch_computations={%region_16.0_spmd, %region_17.0_spmd, %region_18.0_spmd, %region_1... | conditional | bytes 8 | solution.py:471
  114.0 35.4 %round_col13.1 = (f32[512,512]{1,0:T(8,128)}, f32[512,512]{1,0:T(8,128)}, bf16[512,512]{1,0:T(8,128)(2,1)}, bf16[512,512]{1,0:T(8,128)(2,1)}) custom-call(s32[1]{0:T(128)} %get-tuple-element.896.lap_ref, f32[512,512]{1,0:T(8,128)S(1)} %get-tuple-element.897.ctx_ref, f32[512,512]{1,0:T(8,128)S(1)} %get-tuple-element.898.src_in, ...), custom_call_target="tpu_custom_call" | custom-call | tf_op jit(solution)/shard_map/while/body/eval_jaxpr/cond/branch_12_fun/round_col13/pallas_call | solution.py:241
  149.6 75.7 %conditional.3 = ((f32[512,512]{1,0:T(8,128)S(1)}, f32[512,512]{1,0:T(8,128)S(1)})) conditional(s32[]{:T(128)} %clamp.31, (s32[1]{0:T(128)}, f32[512,512]{1,0:T(8,128)}, f32[512,512]{1,0:T(8,128)}, bf16[512,512]{1,0:T(8,128)(2,1)}, bf16[512,512]{1,0:T(8,128)(2,1)}) %tuple.172, (s32[1]{0:T(128)}, ...), branch_computations={%region_32.33_spmd, %region_33.34_spmd, %region_34.35_spmd, %regio... | conditional | bytes 8 | solution.py:486
  149.6 75.6 %home9.1 = (f32[512,512]{1,0:T(8,128)S(1)}, f32[512,512]{1,0:T(8,128)S(1)}) custom-call(s32[1]{0:T(128)} %get-tuple-element.975.total, f32[512,512]{1,0:T(8,128)} %get-tuple-element.976.ctx_ref, f32[512,512]{1,0:T(8,128)} %get-tuple-element.977.src_in, bf16[512,512]{1,0:T(8,128)(2,1)} %get-tuple-element.978.coef_in, bf16[512,512]{1,0:T(8,128)(2,1)} %get-tuple-element.979.low_in), custom_call_target="tpu_custom_call" | custom-call | tf_op jit(solution)/shard_map/cond/branch_9_fun/home9/pallas_call | solution.py:445
  225.3 1.0 copy.179
  226.3 1.0 copy.180
Async XLA Ops:
  0.6 4.6 %copy-start = (s32[4]{0:T(128)S(1)}, s32[4]{0:T(128)}, u32[]{:S(2)}) copy-start(s32[4]{0:T(128)} %param.55) | copy-start | bytes 52

commit v2 on v1

--- a/solution.py
+++ b/solution.py
@@ -270,7 +270,7 @@
     return detour if detour.any else None
 
 
-def return_kernel(by, total, ctx_ref, src_in, coef_in, low_in, ctx_out, src_out, *scratch):
+def return_kernel(by, offsets, ctx_ref, src_in, coef_in, low_in, ctx_out, src_out, *scratch):
     near = scratch[:QUARTERS]
     stage = scratch[QUARTERS : 2 * QUARTERS]
     far = scratch[2 * QUARTERS : 3 * QUARTERS]
@@ -404,7 +404,10 @@
             tiles(COLS // 2, lambda k: relay(q, part, part * (COLS // 2) + k).start())
 
         tiles(flag, pass_relay)
-    shift = total[0]
+    shift = offsets[1]
+    for turn in range(3, offsets.shape[0], 2):
+        shift = shift + offsets[turn]
+    shift = lax.rem(shift, COLS)
     for q in range(QUARTERS):
         spread_all(q).wait_recv()
         far[q][0] = near[q][lax.rem(shift, COLS)]
@@ -429,7 +432,7 @@
         tiles(flag, lambda i, q=q, part=part: relayed(q, part).wait_send())
 
 
-def go_home(by, number, total, ctx, src, coef, low):
+def go_home(by, number, offsets, ctx, src, coef, low):
     size, width = ctx.shape
     quarter = size // QUARTERS
     vmem = pl.BlockSpec(memory_space=pltpu.VMEM)
@@ -454,13 +457,52 @@
         compiler_params=pltpu.CompilerParams(
             collective_id=number, has_side_effects=True, vmem_limit_bytes=24 << 20
         ),
-    )(total, ctx, src, coef, low)
+    )(offsets, ctx, src, coef, low)
+
+
+def open_kernel(ctx_ref, src_ref, ctx_out, src_out, coef_out, low_out, sems):
+    copies = [
+        pltpu.make_async_copy(ctx_ref, ctx_out, sems.at[0]),
+        pltpu.make_async_copy(src_ref, src_out, sems.at[1]),
+    ]
+    for copy in copies:
+        copy.start()
+
+    def clear(i):
+        rows = block(i, STRIP)
+        coef_out[rows, :] = jnp.zeros((STRIP, coef_out.shape[1]), coef_out.dtype)
+        low_out[rows, :] = jnp.zeros((STRIP, low_out.shape[1]), low_out.dtype)
+
+    tiles(coef_out.shape[0] // STRIP, clear)
+    for copy in copies:
+        copy.wait()
+
+
+def opened(ctx, src):
+    vmem = pl.BlockSpec(memory_space=pltpu.VMEM)
+    hbm = pl.BlockSpec(memory_space=pl.ANY)
+    return pl.pallas_call(
+        open_kernel,
+        out_shape=(
+            jax.ShapeDtypeStruct(ctx.shape, ctx.dtype),
+            jax.ShapeDtypeStruct(src.shape, src.dtype),
+            jax.ShapeDtypeStruct((src.shape[0], ctx.shape[0]), jnp.bfloat16),
+            jax.ShapeDtypeStruct(ctx.shape, jnp.bfloat16),
+        ),
+        in_specs=[hbm, hbm],
+        out_specs=[pl.BlockSpec(memory_space=pltpu.VMEM), pl.BlockSpec(memory_space=pltpu.VMEM), vmem, vmem],
+        scratch_shapes=[pltpu.SemaphoreType.DMA((2,))],
+        name="opened",
+    )(ctx, src)
 
 
 def per_device(source, context, pair_counts, partner_masks):
     rounds = pair_counts.shape[0]
 
+    picks = partner_masks - 1
+
     def both(lap, carried):
+        pair = lax.dynamic_slice_in_dim(picks, 2 * lap, 2, allow_negative_indices=False)
         for half, (axis, length) in enumerate((("row", ROWS), ("col", COLS))):
             branches = [
                 functools.partial(
@@ -468,22 +510,13 @@
                 )
                 for by in range(1, length)
             ]
-            carried = lax.switch(
-                partner_masks[2 * lap + half] - 1,
-                branches,
-                lap.reshape(1),
-                *carried,
-                pair_counts,
-            )
+            carried = lax.switch(pair[half], branches, lap.reshape(1), *carried, pair_counts)
         return tuple(carried)
 
-    coef = jnp.zeros((source.shape[0], context.shape[0]), jnp.bfloat16)
-    low = jnp.zeros(context.shape, jnp.bfloat16)
-    ctx, src, coef, low = lax.fori_loop(0, rounds // 2, both, (context, source, coef, low))
-    row_total = sum(partner_masks[turn] for turn in range(0, rounds, 2)) % ROWS
-    col_total = sum(partner_masks[turn] for turn in range(1, rounds, 2)) % COLS
+    ctx, src, coef, low = lax.fori_loop(0, rounds // 2, both, opened(context, source))
+    row_total = sum(partner_masks[turn] for turn in range(0, rounds, 2)) & (ROWS - 1)
     branches = [functools.partial(go_home, by, 2 * ROWS + by) for by in range(ROWS)]
-    ctx, src = lax.switch(row_total, branches, col_total.reshape(1), ctx, src, coef, low)
+    ctx, src = lax.switch(row_total, branches, partner_masks, ctx, src, coef, low)
     return (src, ctx)
 
 

time: 227 us -> 213 us (0.938)
  Pallas kernels: 211 us -> 203 us
  local copies, waits for them, and re-layouts: 10 us -> 3.97 us
    pallas_call x1, Pallas kernels: 75.6 us -> 51.7 us  [go_home(): pl.pallas_call(functools.partial(return_kernel, by), out_shape=(full, ful...]
    pallas_call x4, Pallas kernels: 136 us -> 148 us  [one_round(): pl.pallas_call(functools.partial(round_kernel, axis, by, turns), out_shap...]
    unnamed x6 -> x4, local copies, waits for them, and re-layouts: 6.51 us -> 1.95 us
    pallas_call x0 -> x1, Pallas kernels: none -> 3.21 us  [opened(): pl.pallas_call(open_kernel, out_shape=(jax.ShapeDtypeStruct(ctx.shape, ct...]
where the time goes in v2:
time: 213 us
  Pallas kernels  203 us (95%)
  local copies, waits for them, and re-layouts  3.97 us (2%)
  loops' own time  3.07 us (1%)
    pallas_call x4, Pallas kernels, one_round(): pl.pallas_call(functools.partial(round_kernel, axis, by, turns), out_shap...  148 us
    pallas_call x1, Pallas kernels, go_home(): pl.pallas_call(functools.partial(return_kernel, by), out_shape=(full, ful...  51.7 us

profile of v2, /device:TPU:1, one launch (start us, length us, event | category | flops | bytes accessed | tf_op | source)
XLA Modules:
  0.0 213.1 jit_solution(9720047600311599469)
XLA Ops:
  0.6 3.2 %opened.1 = (f32[512,512]{1,0:T(8,128)}, f32[512,512]{1,0:T(8,128)}, bf16[512,512]{1,0:T(8,128)(2,1)}, bf16[512,512]{1,0:T(8,128)(2,1)}) custom-call(f32[512,512]{1,0:T(8,128)} %ctx_ref.1, f32[512,512]{1,0:T(8,128)} %src_ref.1), custom_call_target="tpu_custom_call" | custom-call | tf_op jit(solution)/shard_map/opened/pallas_call | solution.py:484
  3.8 0.7 broadcast_add_fusion
  4.5 0.0 copy-start
  4.5 152.9 %while.19 = (s32[]{:T(128)}, f32[512,512]{1,0:T(8,128)}, f32[512,512]{1,0:T(8,128)}, bf16[512,512]{1,0:T(8,128)(2,1)}, bf16[512,512]{1,0:T(8,128)(2,1)}, /*index...) while((s32[]{:T(128)}, f32[512,512]{1,0:T(8,128)}, ...), condition=%wide.region_31.0_spmd, body=%wide.region_0.0_spmd.sunk | while | flops 5 | bytes 301 | solution.py:516
  4.5 0.1 dynamic_slice.8
  4.6 0.6 fusion.3
  5.9 57.9 %conditional.6 = ((f32[512,512]{1,0:T(8,128)S(1)}, f32[512,512]{1,0:T(8,128)S(1)}, bf16[512,512]{1,0:T(8,128)(2,1)S(1)}, bf16[512,512]{1,0:T(8,128)(2,1)S(1)})) conditional(s32[]{:T(128)} %bitcast.9, (s32[1]{0:T(128)}, f32[512,512]{1,0:T(8,128)}, f32[512,512]{1,0:T(8,128)}, bf16[512,512]{1,0:T(8,128)(2,1)}, ...), branch_computations={%region_1.0_spmd, %region_2.0_spmd, %region_3.0_spmd, %region_4.0_... | conditional | bytes 8 | solution.py:513
  5.9 57.9 %round_row11.1 = (f32[512,512]{1,0:T(8,128)S(1)}, f32[512,512]{1,0:T(8,128)S(1)}, bf16[512,512]{1,0:T(8,128)(2,1)S(1)}, bf16[512,512]{1,0:T(8,128)(2,1)S(1)}) custom-call(s32[1]{0:T(128)} %get-tuple-element.703.lap_ref, f32[512,512]{1,0:T(8,128)} %get-tuple-element.704.ctx_ref, f32[512,512]{1,0:T(8,128)} %get-tuple-element.705.src_in, ...), custom_call_target="tpu_custom_call" | custom-call | tf_op jit(solution)/shard_map/while/body/eval_jaxpr/cond/branch_10_fun/round_row11/pallas_call | solution.py:241
  64.4 17.0 %conditional.7 = ((f32[512,512]{1,0:T(8,128)}, f32[512,512]{1,0:T(8,128)}, bf16[512,512]{1,0:T(8,128)(2,1)}, bf16[512,512]{1,0:T(8,128)(2,1)})) conditional(s32[]{:T(128)} %bitcast.7, (s32[1]{0:T(128)}, f32[512,512]{1,0:T(8,128)S(1)}, f32[512,512]{1,0:T(8,128)S(1)}, bf16[512,512]{1,0:T(8,128)(2,1)S(1)}, ...), branch_computations={%region_16.0_spmd, %region_17.0_spmd, %region_18.0_spmd, %region_1... | conditional | bytes 8 | solution.py:513
  64.5 17.0 %round_col15.1 = (f32[512,512]{1,0:T(8,128)}, f32[512,512]{1,0:T(8,128)}, bf16[512,512]{1,0:T(8,128)(2,1)}, bf16[512,512]{1,0:T(8,128)(2,1)}) custom-call(s32[1]{0:T(128)} %get-tuple-element.817.lap_ref, f32[512,512]{1,0:T(8,128)S(1)} %get-tuple-element.818.ctx_ref, f32[512,512]{1,0:T(8,128)S(1)} %get-tuple-element.819.src_in, ...), custom_call_target="tpu_custom_call" | custom-call | tf_op jit(solution)/shard_map/while/body/eval_jaxpr/cond/branch_14_fun/round_col15/pallas_call | solution.py:241
  81.5 0.1 dynamic_slice.8
  81.6 0.6 fusion.3
  82.9 47.3 %conditional.6 = ((f32[512,512]{1,0:T(8,128)S(1)}, f32[512,512]{1,0:T(8,128)S(1)}, bf16[512,512]{1,0:T(8,128)(2,1)S(1)}, bf16[512,512]{1,0:T(8,128)(2,1)S(1)})) conditional(s32[]{:T(128)} %bitcast.9, (s32[1]{0:T(128)}, f32[512,512]{1,0:T(8,128)}, f32[512,512]{1,0:T(8,128)}, bf16[512,512]{1,0:T(8,128)(2,1)}, ...), branch_computations={%region_1.0_spmd, %region_2.0_spmd, %region_3.0_spmd, %region_4.0_... | conditional | bytes 8 | solution.py:513
  82.9 47.2 %round_row7.1 = (f32[512,512]{1,0:T(8,128)S(1)}, f32[512,512]{1,0:T(8,128)S(1)}, bf16[512,512]{1,0:T(8,128)(2,1)S(1)}, bf16[512,512]{1,0:T(8,128)(2,1)S(1)}) custom-call(s32[1]{0:T(128)} %get-tuple-element.679.lap_ref, f32[512,512]{1,0:T(8,128)} %get-tuple-element.680.ctx_ref, f32[512,512]{1,0:T(8,128)} %get-tuple-element.681.src_in, ...), custom_call_target="tpu_custom_call" | custom-call | tf_op jit(solution)/shard_map/while/body/eval_jaxpr/cond/branch_6_fun/round_row7/pallas_call | solution.py:241
  130.8 26.5 %conditional.7 = ((f32[512,512]{1,0:T(8,128)}, f32[512,512]{1,0:T(8,128)}, bf16[512,512]{1,0:T(8,128)(2,1)}, bf16[512,512]{1,0:T(8,128)(2,1)})) conditional(s32[]{:T(128)} %bitcast.7, (s32[1]{0:T(128)}, f32[512,512]{1,0:T(8,128)S(1)}, f32[512,512]{1,0:T(8,128)S(1)}, bf16[512,512]{1,0:T(8,128)(2,1)S(1)}, ...), branch_computations={%region_16.0_spmd, %region_17.0_spmd, %region_18.0_spmd, %region_1... | conditional | bytes 8 | solution.py:513
  130.8 26.4 %round_col7.1 = (f32[512,512]{1,0:T(8,128)}, f32[512,512]{1,0:T(8,128)}, bf16[512,512]{1,0:T(8,128)(2,1)}, bf16[512,512]{1,0:T(8,128)(2,1)}) custom-call(s32[1]{0:T(128)} %get-tuple-element.769.lap_ref, f32[512,512]{1,0:T(8,128)S(1)} %get-tuple-element.770.ctx_ref, f32[512,512]{1,0:T(8,128)S(1)} %get-tuple-element.771.src_in, ...), custom_call_target="tpu_custom_call" | custom-call | tf_op jit(solution)/shard_map/while/body/eval_jaxpr/cond/branch_6_fun/round_col7/pallas_call | solution.py:241
  157.4 0.0 copy-done
  157.5 0.6 fusion.1
  159.3 51.8 %conditional.3 = ((f32[512,512]{1,0:T(8,128)S(1)}, f32[512,512]{1,0:T(8,128)S(1)})) conditional(s32[]{:T(128)} %bitcast.3, (s32[4]{0:T(128)S(1)}, f32[512,512]{1,0:T(8,128)}, f32[512,512]{1,0:T(8,128)}, bf16[512,512]{1,0:T(8,128)(2,1)}, bf16[512,512]{1,0:T(8,128)(2,1)}) %tuple.276, (s32[4]{0:T(128)S(1)}, ...), branch_computations={%region_32.0_spmd, %region_33.0_spmd, %region_34.0_spmd, %region_3... | conditional | bytes 8 | solution.py:519
  159.4 51.7 %home2.1 = (f32[512,512]{1,0:T(8,128)S(1)}, f32[512,512]{1,0:T(8,128)S(1)}) custom-call(s32[4]{0:T(128)S(1)} %get-tuple-element.849.offsets, f32[512,512]{1,0:T(8,128)} %get-tuple-element.850.ctx_ref, f32[512,512]{1,0:T(8,128)} %get-tuple-element.851.src_in, bf16[512,512]{1,0:T(8,128)(2,1)} %get-tuple-element.852.coef_in, ...), custom_call_target="tpu_custom_call" | custom-call | tf_op jit(solution)/shard_map/cond/branch_2_fun/home2/pallas_call | solution.py:448
  211.1 1.0 copy.177
  212.1 1.0 copy.178
Async XLA Ops:
  4.5 152.9 %copy-start = (s32[4]{0:T(128)S(1)}, s32[4]{0:T(128)}, u32[]{:S(2)}) copy-start(s32[4]{0:T(128)} %param.55) | copy-start | bytes 52
